TPU v7x, 256 devices: a whole 4x4x8 slice. The times are simulated.
256 devices in a mesh: gx: 16 (over z, core), gy: 16 (over y, x).
Axes of the slice: x: 4, y: 4, z: 8, core: 2. Of those that a mesh axis runs over, the one named last changes fastest.
Arguments:
- modes: float32 [524288, 512], P(('gx', 'gy'))
- batch: float32 [524288, 256], P(('gx', 'gy')), as said below
- core: float32 [768, 512], replicated, may hold values from -0.21875 to 0.21875
Outputs:
- new_modes: float32 [524288, 512], P(('gx', 'gy'))
Inputs may be any that keep to these rules, and one draw needn't show every extreme that they name: Each row of modes and batch shares one positive scale; batch holds a sizeable part of the span of modes.
All inputs are finite; a program needn't handle non-finite values.
Results may differ from a plain program's by a relative error of at most 0.000058.
Values sent between devices are 32-bit elements; how exact they have to be, the bound alone decides.
A program may use at most 64 MiB of HBM per device.

v0:
```python
import jax
import jax.numpy as jnp
from jax import lax
from jax.sharding import PartitionSpec as P


def matmul(left, right):
    return jnp.dot(left, right, precision=lax.Precision.HIGHEST, preferred_element_type=jnp.float32)


def global_sum(parts):
    return lax.psum((parts[0],), ("gx", "gy"))


def shards(modes, batch, core):
    total_rows = modes.shape[0] * lax.axis_size("gx") * lax.axis_size("gy")
    width = modes.shape[1]
    top = matmul(modes, core[:width])
    cross = global_sum((matmul(modes.T, batch),))[0]
    coeffs = cross / total_rows
    resid = batch - matmul(modes, coeffs)
    gram = global_sum((matmul(resid.T, resid),))[0] / total_rows
    lower = jnp.linalg.cholesky(gram)
    basis = jax.scipy.linalg.solve_triangular(lower, resid.T, lower=True).T
    return top + matmul(basis, core[width:])


def solution(mesh):
    placed = (P(("gx", "gy"), None), P(("gx", "gy"), None), P())
    return jax.shard_map(
        shards, mesh=mesh, in_specs=placed, out_specs=P(("gx", "gy"), None), check_vma=False
    )
```

profile of v0, /device:TPU:2, one launch (start us, length us, event | category | flops | bytes accessed | tf_op | source)
XLA Modules:
  0.0 619.7 jit_solution(16031329301337902461)
XLA Ops:
  6.5 0.0 copy-start.1
  6.5 0.0 all-reduce.4.cloned.1.call-start
  6.5 10.5 %fusion.20 = f32[512,256]{1,0:T(8,128)} fusion(f32[2048,512]{1,0:T(8,128)} %param.3, f32[2048,256]{1,0:T(8,128)} %param.4), kind=kOutput, calls=%fused_computation.42 | convolution fusion | flops 3221225472 | bytes 6815744 | tf_op jit(solution)/shard_map/dot_general | solution.py:8
  17.0 0.0 all-reduce.4.cloned.1.call-update
  17.0 0.5 all-reduce.6.cloned.1.call-start
  17.6 0.0 copy-done.1
  17.6 1.8 copy.4
  19.4 256.1 %all-reduce.4.cloned.1.call-done = f32[512,256]{1,0:T(8,128)} async-done(((f32[512,256]{1,0:T(8,128)}), f32[512,256]{1,0:T(8,128)}) %all-reduce.4.cloned.1.call-update) | async-done | bytes 524304 | tf_op jit(solution)/shard_map/psum | solution.py:12
  275.5 9.9 %fusion = f32[2048,256]{0,1:T(8,128)S(1)} fusion(f32[2048,256]{0,1:T(8,128)} %copy.4, f32[2048,512]{1,0:T(8,128)} %param.3, f32[512,256]{1,0:T(8,128)} %all-reduce.4.cloned.1.call-done), kind=kOutput, calls=%fused_computation.4 | convolution fusion | flops 3221880832 | bytes 8912896 | tf_op jit(solution)/shard_map/dot_general | solution.py:8
  285.5 2.6 fusion.21
  288.0 0.0 all-reduce.6.cloned.1.call-update
  288.1 10.2 %fusion.6 = f32[2048,512]{1,0:T(8,128)} fusion(f32[2048,512]{1,0:T(8,128)} %param.3, f32[768,512]{1,0:T(8,128)} %param.5), kind=kOutput, calls=%fused_computation.12 | convolution fusion | flops 6442450944 | bytes 9437184 | tf_op jit(solution)/shard_map/dot_general | solution.py:8
  298.3 242.9 %all-reduce.6.cloned.1.call-done = f32[256,256]{0,1:T(8,128)} async-done(((f32[256,256]{0,1:T(8,128)}), f32[256,256]{0,1:T(8,128)}) %all-reduce.6.cloned.1.call-update) | async-done | bytes 262160 | tf_op jit(solution)/shard_map/psum | solution.py:12
  541.2 1.0 broadcast_multiply_fusion
  542.2 0.1 copy.6
  542.3 1.0 fusion.10
  543.3 11.7 %cholesky.50 = f32[128,128]{1,0:T(8,128)S(1)} custom-call(f32[128,128]{1,0:T(8,128)S(1)} %cholesky.118), custom_call_target="Cholesky" | custom-call | tf_op jit(solution)/shard_map/jit(cholesky)/cholesky | solution.py:23
  555.0 9.8 %custom-call.15 = f32[1,128,128]{1,2,0:T(8,128)S(1)} custom-call(f32[1,128,128]{2,1,0:T(8,128)S(1)} %get-tuple-element.26), custom_call_target="InvertDiagBlocksLowerTriangular" | custom-call | tf_op jit(solution)/shard_map/jit(cholesky)/cholesky | solution.py:23
  564.9 0.2 constant_dynamic-update-slice_fusion.1
  565.1 0.3 convolution_subtract_fusion.1
  565.4 11.7 %cholesky.105 = f32[128,128]{1,0:T(8,128)S(1)} custom-call(f32[128,128]{1,0:T(8,128)S(1)} %convolution_subtract_fusion.1), custom_call_target="Cholesky" | custom-call | tf_op jit(solution)/shard_map/jit(cholesky)/cholesky | solution.py:23
  577.1 0.7 compare_reduce_fusion
  579.1 0.1 triangular_solve.57
  579.2 4.1 while.1
  579.2 0.7 fusion.33
  579.9 1.3 bitcast_dynamic-update-slice_fusion.2
  581.2 0.7 fusion.33
  581.9 1.3 bitcast_dynamic-update-slice_fusion.2
  583.3 19.9 %custom-call.16 = f32[2,128,128]{1,2,0:T(8,128)S(1)} custom-call(f32[2,128,128]{2,1,0:T(8,128)S(1)} %get-tuple-element.12), custom_call_target="InvertDiagBlocksLowerTriangular" | custom-call | tf_op jit(solution)/shard_map/jit(_solve_triangular)/triangular_solve | solution.py:24
  603.2 1.1 fusion.4
  604.2 0.0 copy-start
  604.2 1.0 convolution_subtract_fusion
  605.2 1.1 fusion.13
  606.3 0.1 copy-done
  606.4 6.2 %convolution_add_fusion = f32[2048,512]{1,0:T(8,128)} fusion(f32[2048,512]{1,0:T(8,128)S(1)} %copy-done, f32[128,2048]{1,0:T(8,128)S(1)} %fusion.13, f32[128,2048]{1,0:T(8,128)S(1)} %fusion.4, f32[768,512]{1,0:T(8,128)} %param.5), kind=kOutput, calls=%fused_computation.2 | convolution fusion | flops 3222798336 | bytes 11010048 | tf_op jit(solution)/shard_map/dot_general | solution.py:8
  (9 shorter events, 0.1 us)
Async XLA Ops:
  6.5 11.0 %copy-start.1 = (f32[2048,256]{1,0:T(8,128)S(1)}, f32[2048,256]{1,0:T(8,128)}, u32[]{:S(2)}) copy-start(f32[2048,256]{1,0:T(8,128)} %param.4) | copy-start | bytes 6291460
  6.5 269.0 %all-reduce.4.cloned.1.call-start = ((), (), s32[]{:S(2)}) async-start(), calls=%async_computation | async-start | bytes 1048576 | tf_op jit(solution)/shard_map/psum | solution.py:12
  17.0 524.1 %all-reduce.6.cloned.1.call-start = ((), (), s32[]{:S(2)}) async-start(), calls=%async_computation.1 | async-start | bytes 524288 | tf_op jit(solution)/shard_map/psum | solution.py:12
  604.2 2.2 copy-start
Sparse Core Ops, SparseCore 0:
  17.2 258.3 all-reduce.3
  288.2 252.9 all-reduce.5
where the time goes:
time: 625 us; the launch traced here: 620 us
  waiting for transfers between devices  499 us (80%)
  other arithmetic  55.9 us (9%)
  matrix products  43 us (7%)
  between operations  15 us (2%)
    psum x2, waiting for transfers between devices, global_sum(): return lax.psum((parts[0],), ('gx', 'gy'))  499 us
    dot_general x5, matrix products, matmul(): jnp.dot(left, right, precision=lax.Precision.HIGHEST, preferred_element_t...  39.5 us
    another operation x6, other arithmetic, shards(): lower = jnp.linalg.cholesky(gram)  34 us
    another operation x3, other arithmetic, shards(): basis = jax.scipy.linalg.solve_triangular(lower, resid.T, lower=True).T  19.9 us
  transfers between devices with their start and end apart: 2, of which 2 were waited for; matrix products, arithmetic and copies ran while one was open for 2% of the time, Pallas kernels for 0%

commit v1 on v0

--- a/solution.py
+++ b/solution.py
@@ -1,7 +1,15 @@
+import functools
 import jax
 import jax.numpy as jnp
 from jax import lax
 from jax.sharding import PartitionSpec as P
+
+
+def _meet_vector(array_here, mesh_name, chip_axis):
+    return lax.psum(lax.psum(array_here, mesh_name), chip_axis)
+
+
+define_lines = functools.partial(_meet_vector, mesh_name="gx", chip_axis="gy")
 
 
 def matmul(left, right):
@@ -9,7 +17,7 @@
 
 
 def global_sum(parts):
-    return lax.psum((parts[0],), ("gx", "gy"))
+    return define_lines((parts[0],))
 
 
 def shards(modes, batch, core):

time: 625 us -> 534 us (0.85)
  waiting for transfers between devices: 499 us -> 408 us
    psum x2 -> x4, waiting for transfers between devices: 499 us -> 408 us  [_meet_vector(): return lax.psum(lax.psum(array_here, mesh_name), chip_axis)]
  transfers between devices with their start and end apart: 2 -> 4, of which waited for: 2 -> 4; matrix products, arithmetic and copies ran while one was open for 2% -> 2% of each run, Pallas kernels for 0% -> 0%
where the time goes in v1:
time: 534 us; the launch traced here: 529 us
  waiting for transfers between devices  408 us (76%)
  other arithmetic  55.9 us (10%)
  matrix products  43 us (8%)
  between operations  14.8 us (3%)
  local copies, waits for them, and re-layouts  6.17 us (1%)
    psum x4, waiting for transfers between devices, _meet_vector(): return lax.psum(lax.psum(array_here, mesh_name), chip_axis)  408 us
    dot_general x5, matrix products, matmul(): jnp.dot(left, right, precision=lax.Precision.HIGHEST, preferred_element_t...  39.4 us
    another operation x6, other arithmetic, shards(): lower = jnp.linalg.cholesky(gram)  34 us
    another operation x3, other arithmetic, shards(): basis = jax.scipy.linalg.solve_triangular(lower, resid.T, lower=True).T  19.9 us
  transfers between devices with their start and end apart: 4, of which 4 were waited for; matrix products, arithmetic and copies ran while one was open for 2% of the time, Pallas kernels for 0%

profile of v1, /device:TPU:2, one launch (start us, length us, event | category | flops | bytes accessed | tf_op | source)
XLA Modules:
  0.0 528.9 jit_solution(4050120570851998627)
XLA Ops:
  6.5 0.0 all-reduce.6.cloned.1.call-start
  6.5 0.0 copy-start.1
  6.5 10.5 %fusion.20 = f32[512,256]{1,0:T(8,128)} fusion(f32[2048,512]{1,0:T(8,128)} %param.3, f32[2048,256]{1,0:T(8,128)} %param.4), kind=kOutput, calls=%fused_computation.42 | convolution fusion | flops 3221225472 | bytes 6815744 | tf_op jit(solution)/shard_map/dot_general | solution.py:16
  17.0 0.0 all-reduce.6.cloned.1.call-update
  17.0 0.0 all-reduce.8.cloned.1.call-start
  17.1 113.8 %all-reduce.6.cloned.1.call-done = f32[512,256]{1,0:T(8,128)} async-done(((f32[512,256]{1,0:T(8,128)}), f32[512,256]{1,0:T(8,128)}) %all-reduce.6.cloned.1.call-update) | async-done | bytes 524304 | tf_op jit(solution)/shard_map/psum | solution.py:9
  130.9 0.0 all-reduce.8.cloned.1.call-update
  130.9 0.5 all-reduce.10.cloned.1.call-start
  131.4 0.0 copy-done.1
  131.4 1.8 copy.4
  133.2 96.8 %all-reduce.8.cloned.1.call-done = f32[512,256]{1,0:T(8,128)} async-done(((f32[512,256]{1,0:T(8,128)}), f32[512,256]{1,0:T(8,128)}) %all-reduce.8.cloned.1.call-update) | async-done | bytes 524304 | tf_op jit(solution)/shard_map/psum | solution.py:9
  230.0 9.9 %fusion = f32[2048,256]{0,1:T(8,128)S(1)} fusion(f32[2048,256]{0,1:T(8,128)} %copy.4, f32[2048,512]{1,0:T(8,128)} %param.3, f32[512,256]{1,0:T(8,128)} %all-reduce.8.cloned.1.call-done), kind=kOutput, calls=%fused_computation.4 | convolution fusion | flops 3221880832 | bytes 8912896 | tf_op jit(solution)/shard_map/dot_general | solution.py:16
  239.9 2.6 fusion.21
  242.5 0.0 all-reduce.10.cloned.1.call-update
  242.5 0.0 all-reduce.12.cloned.1.call-start
  242.6 109.9 %all-reduce.10.cloned.1.call-done = f32[256,256]{0,1:T(8,128)} async-done(((f32[256,256]{0,1:T(8,128)}), f32[256,256]{0,1:T(8,128)}) %all-reduce.10.cloned.1.call-update) | async-done | bytes 262160 | tf_op jit(solution)/shard_map/psum | solution.py:9
  352.4 0.0 all-reduce.12.cloned.1.call-update
  352.4 10.2 %fusion.6 = f32[2048,512]{1,0:T(8,128)} fusion(f32[2048,512]{1,0:T(8,128)} %param.3, f32[768,512]{1,0:T(8,128)} %param.5), kind=kOutput, calls=%fused_computation.12 | convolution fusion | flops 6442450944 | bytes 9437184 | tf_op jit(solution)/shard_map/dot_general | solution.py:16
  362.7 88.0 %all-reduce.12.cloned.1.call-done = f32[256,256]{0,1:T(8,128)} async-done(((f32[256,256]{0,1:T(8,128)}), f32[256,256]{0,1:T(8,128)}) %all-reduce.12.cloned.1.call-update) | async-done | bytes 262160 | tf_op jit(solution)/shard_map/psum | solution.py:9
  450.7 1.0 broadcast_multiply_fusion
  451.7 0.1 copy.6
  451.8 1.0 fusion.10
  452.8 11.7 %cholesky.50 = f32[128,128]{1,0:T(8,128)S(1)} custom-call(f32[128,128]{1,0:T(8,128)S(1)} %cholesky.118), custom_call_target="Cholesky" | custom-call | tf_op jit(solution)/shard_map/jit(cholesky)/cholesky | solution.py:31
  464.5 9.8 %custom-call.15 = f32[1,128,128]{1,2,0:T(8,128)S(1)} custom-call(f32[1,128,128]{2,1,0:T(8,128)S(1)} %get-tuple-element.26), custom_call_target="InvertDiagBlocksLowerTriangular" | custom-call | tf_op jit(solution)/shard_map/jit(cholesky)/cholesky | solution.py:31
  474.4 0.2 constant_dynamic-update-slice_fusion.1
  474.6 0.3 convolution_subtract_fusion.1
  474.9 11.7 %cholesky.105 = f32[128,128]{1,0:T(8,128)S(1)} custom-call(f32[128,128]{1,0:T(8,128)S(1)} %convolution_subtract_fusion.1), custom_call_target="Cholesky" | custom-call | tf_op jit(solution)/shard_map/jit(cholesky)/cholesky | solution.py:31
  486.6 0.7 compare_reduce_fusion
  488.6 0.1 triangular_solve.57
  488.7 4.1 while.1
  488.7 0.7 fusion.33
  489.4 1.3 bitcast_dynamic-update-slice_fusion.2
  490.7 0.7 fusion.33
  491.4 1.3 bitcast_dynamic-update-slice_fusion.2
  492.8 19.9 %custom-call.16 = f32[2,128,128]{1,2,0:T(8,128)S(1)} custom-call(f32[2,128,128]{2,1,0:T(8,128)S(1)} %get-tuple-element.12), custom_call_target="InvertDiagBlocksLowerTriangular" | custom-call | tf_op jit(solution)/shard_map/jit(_solve_triangular)/triangular_solve | solution.py:32
  512.7 1.1 fusion.4
  513.7 0.0 copy-start
  513.7 1.0 convolution_subtract_fusion
  514.8 1.1 fusion.13
  515.8 0.1 copy-done
  515.9 6.2 %convolution_add_fusion = f32[2048,512]{1,0:T(8,128)} fusion(f32[2048,512]{1,0:T(8,128)S(1)} %copy-done, f32[128,2048]{1,0:T(8,128)S(1)} %fusion.13, f32[128,2048]{1,0:T(8,128)S(1)} %fusion.4, f32[768,512]{1,0:T(8,128)} %param.5), kind=kOutput, calls=%fused_computation.2 | convolution fusion | flops 3222798336 | bytes 11010048 | tf_op jit(solution)/shard_map/dot_general | solution.py:16
  (9 shorter events, 0.1 us)
Async XLA Ops:
  6.5 124.3 %all-reduce.6.cloned.1.call-start = ((), (), s32[]{:S(2)}) async-start(), calls=%async_computation | async-start | bytes 1048576 | tf_op jit(solution)/shard_map/psum | solution.py:9
  6.5 124.9 %copy-start.1 = (f32[2048,256]{1,0:T(8,128)S(1)}, f32[2048,256]{1,0:T(8,128)}, u32[]{:S(2)}) copy-start(f32[2048,256]{1,0:T(8,128)} %param.4) | copy-start | bytes 6291460
  17.0 212.9 %all-reduce.8.cloned.1.call-start = ((), (), s32[]{:S(2)}) async-start(), calls=%async_computation.1 | async-start | bytes 1048576 | tf_op jit(solution)/shard_map/psum | solution.py:9
  130.9 221.5 %all-reduce.10.cloned.1.call-start = ((), (), s32[]{:S(2)}) async-start(), calls=%async_computation.2 | async-start | bytes 524288 | tf_op jit(solution)/shard_map/psum | solution.py:9
  242.5 208.2 %all-reduce.12.cloned.1.call-start = ((), (), s32[]{:S(2)}) async-start(), calls=%async_computation.3 | async-start | bytes 524288 | tf_op jit(solution)/shard_map/psum | solution.py:9
  513.7 2.2 copy-start
Sparse Core Ops, SparseCore 0:
  17.1 113.6 all-reduce.5
  134.1 95.8 all-reduce.7
  242.6 109.7 all-reduce.9
  355.4 95.2 all-reduce.11
